TPU v7x, 32 devices: a whole 2x2x4 slice. The times are simulated.
32 devices in a mesh: vid: 2 (over core), txt: 4 (over y, x), head: 4 (over z).
Axes of the slice: x: 2, y: 2, z: 4, core: 2. Of those that a mesh axis runs over, the one named last changes fastest.
Arguments:
- latents: bfloat16 [32, 128, 768], P('txt', 'vid'), may hold values from -6 to 6
- video_tokens: bfloat16 [32, 1024, 768], P('txt', 'vid'), may hold values from -6 to 6
- caption_tokens: bfloat16 [32, 64, 768], P('vid', 'txt'), may hold values from -6 to 6
- caption_len: int32 [32], P('vid'), may hold values from 5 to 60
- key_mask: int32 [32, 64], P('vid', 'txt'), may hold values 0 or 1
- drop_flags: int32 [32], P('txt'), may hold values 0 or 1
- gain_latent: float32 [768], replicated, may hold values from 0.5 to 1.5
- gain_tokens: float32 [768], replicated, may hold values from 0.5 to 1.5
- gain_mlp: float32 [768], replicated, may hold values from 0.5 to 1.5
- query_weight: bfloat16 [768, 768], P(None, 'head'), may hold values from -0.21875 to 0.21875
- key_matrix: bfloat16 [768, 768], P(None, 'head'), may hold values from -0.21875 to 0.21875
- value_matrix: bfloat16 [768, 768], P(None, 'head'), may hold values from -0.21875 to 0.21875
- out_weight: bfloat16 [768, 768], P('head'), may hold values from -6 to 6
- up_weight: bfloat16 [768, 3072], P(None, 'head'), may hold values from -0.21875 to 0.21875
- down_weight: bfloat16 [3072, 768], P('head'), may hold values from -0.109375 to 0.109375
- cotangent: bfloat16 [32, 128, 768], P('txt', 'vid'), may hold values from -6 to 6
Outputs:
- latents_out: bfloat16 [32, 128, 768], P('txt', 'vid')
- latent_grad: float32 [32, 128, 768], P('txt', 'vid')
- video_grad: float32 [32, 1024, 768], P('txt', 'vid')
- caption_grad: float32 [32, 64, 768], P('vid', 'txt')
- grad_query: float32 [768, 768], P(None, 'head')
- grad_key: float32 [768, 768], P(None, 'head')
- grad_value: float32 [768, 768], P(None, 'head')
- grad_out: float32 [768, 768], P('head')
- grad_up: float32 [768, 3072], P(None, 'head')
- grad_down: float32 [3072, 768], P('head')
- grad_gain_latent: float32 [768], replicated
- grad_gain_tokens: float32 [768], replicated
- grad_gain_mlp: float32 [768], replicated
- kept_count: int32 [], replicated
All inputs are finite; a program needn't handle non-finite values. No bound on the sum of `key_mask` or of `drop_flags` on one device may be relied on, other than what follows from the above.
Results may differ from a plain program's by a relative error of at most 0.012.
Values may be sent and summed in bfloat16 or wider, within the bound.
No kernel may reach another device: no remote copies, remote signals or barrier semaphores. Data moves between devices by JAX's collectives and lax.ppermute only.
A program may use at most 128 MiB of HBM per device.

v0:
```python
import math
import jax
import jax.numpy as jnp
from jax import lax
from jax.sharding import PartitionSpec as P

D = 768
HEADS = 12


def combined_all(part, axis, combine):
    gathered = jax.tree.map(lambda a: lax.all_gather(a, axis), part)

    def take(source):
        return jax.tree.map(lambda a: lax.dynamic_index_in_dim(a, source, 0, False), gathered)

    return lax.fori_loop(
        1, lax.axis_size(axis), lambda source, state: combine(state, take(source)), take(0)
    )


def layer_norm(values, gain):
    center = values - jnp.mean(values, axis=-1, keepdims=True)
    spread = jnp.mean(center * center, axis=-1, keepdims=True)
    return center * lax.rsqrt(spread + 1e-05) * gain


def norm_back(values, gain, upstream):
    result, pullback = jax.vjp(layer_norm, values, gain)
    return pullback(upstream)


def gelu_exact(values):
    return jax.nn.gelu(values, approximate=False)


def combine_stats(first, second):
    peak = jnp.maximum(first[0], second[0])
    total = first[1] * jnp.exp(first[0] - peak) + second[1] * jnp.exp(second[0] - peak)
    return (peak, total)


def to_blocks(whole, vid_count, txt_count):
    items, rows, width = whole.shape
    split = whole.reshape(txt_count, items // txt_count, vid_count, rows // vid_count, width)
    return split.transpose(2, 0, 1, 3, 4).reshape(
        vid_count * txt_count, items // txt_count, rows // vid_count, width
    )


def from_blocks(blocked, vid_count, txt_count):
    count, items_here, rows_here, width = blocked.shape
    split = blocked.reshape(vid_count, txt_count, items_here, rows_here, width)
    return split.transpose(1, 2, 0, 3, 4).reshape(
        txt_count * items_here, vid_count * rows_here, width
    )


def place_sum(whole, part, start):
    current = lax.dynamic_slice_in_dim(whole, start, part.shape[0], 0)
    return lax.dynamic_update_slice_in_dim(whole, current + part, start, 0)


def place_stats(peak_all, total_all, peak, total, start):
    old_peak = lax.dynamic_slice_in_dim(peak_all, start, peak.shape[0], 0)
    old_total = lax.dynamic_slice_in_dim(total_all, start, peak.shape[0], 0)
    new_peak, new_total = combine_stats((old_peak, old_total), (peak, total))
    peak_all = lax.dynamic_update_slice_in_dim(peak_all, new_peak, start, 0)
    total_all = lax.dynamic_update_slice_in_dim(total_all, new_total, start, 0)
    return (peak_all, total_all)


def take_rows(whole, start, count):
    return lax.dynamic_slice_in_dim(whole, start, count, 0)


def local(
    latents,
    video_tokens,
    caption_tokens,
    caption_len,
    key_mask,
    drop_flags,
    gain_latent,
    gain_tokens,
    gain_mlp,
    query_weight,
    key_matrix,
    value_matrix,
    out_weight,
    up_weight,
    down_weight,
    cotangent,
):
    vid_count = lax.axis_size("vid")
    txt_count = lax.axis_size("txt")
    vid_index = lax.axis_index("vid")
    txt_index = lax.axis_index("txt")
    items_here = latents.shape[0]
    cap_items = caption_tokens.shape[0]
    items_total = items_here * txt_count
    head_width = query_weight.shape[1]
    head_size = D // HEADS
    heads_here = head_width // head_size
    scale = 1.0 / math.sqrt(head_size)
    video_here = video_tokens.shape[1]
    cap_here = caption_tokens.shape[1]
    video_start = txt_index * items_here
    cap_start = vid_index * cap_items
    keep = (1 - drop_flags).astype(jnp.float32)
    slots = txt_index * cap_here + jnp.arange(cap_here, dtype=jnp.int32)
    cap_valid = (slots[None, :] < caption_len[:, None]) & (key_mask == 1)
    cap_mask = cap_valid[:, None, None, :]

    def split_heads(values):
        return values.reshape(values.shape[0], values.shape[1], heads_here, head_size)

    lat_float = latents.astype(jnp.float32)
    lat_norm = layer_norm(lat_float, gain_latent).astype(jnp.bfloat16)
    queries = jnp.einsum(
        "bld,de->ble", lat_norm, query_weight, preferred_element_type=jnp.float32
    ).astype(jnp.bfloat16)
    all_queries = from_blocks(
        lax.all_gather(queries[None], ("vid", "txt"), axis=0, tiled=True), vid_count, txt_count
    )
    lat_total = all_queries.shape[1]
    video_queries = take_rows(all_queries, video_start, items_here)
    cap_queries = take_rows(all_queries, cap_start, cap_items)
    video_float = video_tokens.astype(jnp.float32)
    cap_float = caption_tokens.astype(jnp.float32)
    video_normed = layer_norm(video_float, gain_tokens).astype(jnp.bfloat16)
    caption_normed = layer_norm(cap_float, gain_tokens).astype(jnp.bfloat16)
    video_keys = jnp.einsum(
        "flc,co->flo", video_normed, key_matrix, preferred_element_type=jnp.float32
    ).astype(jnp.bfloat16)
    video_values = jnp.einsum(
        "flc,co->flo", video_normed, value_matrix, preferred_element_type=jnp.float32
    ).astype(jnp.bfloat16)
    cap_keys = jnp.einsum(
        "flc,co->flo", caption_normed, key_matrix, preferred_element_type=jnp.float32
    ).astype(jnp.bfloat16)
    cap_values = jnp.einsum(
        "flc,co->flo", caption_normed, value_matrix, preferred_element_type=jnp.float32
    ).astype(jnp.bfloat16)
    video_scores = (
        jnp.einsum(
            "blhe,bkhe->bhlk",
            split_heads(video_queries),
            split_heads(video_keys),
            preferred_element_type=jnp.float32,
        )
        * scale
    )
    cap_scores = (
        jnp.einsum(
            "blhe,bkhe->bhlk",
            split_heads(cap_queries),
            split_heads(cap_keys),
            preferred_element_type=jnp.float32,
        )
        * scale
    )
    cap_scores = jnp.where(cap_mask, cap_scores, -1e30)
    video_peak = jnp.max(video_scores, axis=-1)
    video_total = jnp.sum(jnp.exp(video_scores - video_peak[..., None]), axis=-1)
    cap_peak = jnp.max(cap_scores, axis=-1)
    cap_total = jnp.sum(
        jnp.where(cap_mask, jnp.exp(cap_scores - cap_peak[..., None]), 0.0), axis=-1
    )
    peak_all = jnp.full((items_total, heads_here, lat_total), -1e30, jnp.float32)
    total_all = jnp.zeros((items_total, heads_here, lat_total), jnp.float32)
    peak_all, total_all = place_stats(peak_all, total_all, video_peak, video_total, video_start)
    peak_all, total_all = place_stats(peak_all, total_all, cap_peak, cap_total, cap_start)
    peak, total = combined_all((peak_all, total_all), ("vid", "txt"), combine_stats)
    video_probs = (
        jnp.exp(video_scores - take_rows(peak, video_start, items_here)[..., None])
        / take_rows(total, video_start, items_here)[..., None]
    )
    cap_probs = jnp.where(
        cap_mask,
        jnp.exp(cap_scores - take_rows(peak, cap_start, cap_items)[..., None])
        / take_rows(total, cap_start, cap_items)[..., None],
        0.0,
    )
    video_low = video_probs.astype(jnp.bfloat16)
    cap_low = cap_probs.astype(jnp.bfloat16)
    video_part = jnp.einsum(
        "bhlk,bkhe->blhe", video_low, split_heads(video_values), preferred_element_type=jnp.float32
    ).reshape(items_here, lat_total, head_width)
    cap_part = jnp.einsum(
        "bhlk,bkhe->blhe", cap_low, split_heads(cap_values), preferred_element_type=jnp.float32
    ).reshape(cap_items, lat_total, head_width)
    value_all = jnp.zeros((items_total, lat_total, head_width), jnp.float32)
    value_all = place_sum(place_sum(value_all, video_part, video_start), cap_part, cap_start)
    attended = lax.psum_scatter(
        to_blocks(value_all, vid_count, txt_count), ("vid", "txt"), scatter_dimension=0, tiled=True
    )[0]
    mixed_in = (attended * keep[:, None, None]).astype(jnp.bfloat16)
    branch = lax.psum(
        jnp.einsum("ble,ed->bld", mixed_in, out_weight, preferred_element_type=jnp.float32), "head"
    )
    after_attn = lat_float + branch
    mlp_norm = layer_norm(after_attn, gain_mlp).astype(jnp.bfloat16)
    pre_act = jnp.einsum("bld,df->blf", mlp_norm, up_weight, preferred_element_type=jnp.float32)
    activ = gelu_exact(pre_act).astype(jnp.bfloat16)
    growth = lax.psum(
        jnp.einsum("blf,fd->bld", activ, down_weight, preferred_element_type=jnp.float32).astype(
            jnp.bfloat16
        ),
        "head",
    ).astype(jnp.float32)
    latents_out = (after_attn + growth).astype(jnp.bfloat16)
    grad_down = jnp.einsum("blf,bld->fd", activ, cotangent, preferred_element_type=jnp.float32)
    d_activ = jnp.einsum("bld,fd->blf", cotangent, down_weight, preferred_element_type=jnp.float32)
    d_pre = jax.vjp(gelu_exact, pre_act)[1](d_activ)[0].astype(jnp.bfloat16)
    grad_up = jnp.einsum("bld,blf->df", mlp_norm, d_pre, preferred_element_type=jnp.float32)
    d_mlp_norm = lax.psum(
        jnp.einsum("blf,df->bld", d_pre, up_weight, preferred_element_type=jnp.float32), "head"
    )
    d_after_norm, grad_gain_mlp = norm_back(after_attn, gain_mlp, d_mlp_norm)
    d_after = cotangent.astype(jnp.float32) + d_after_norm
    d_branch = d_after.astype(jnp.bfloat16)
    grad_out = jnp.einsum("ble,bld->ed", mixed_in, d_branch, preferred_element_type=jnp.float32)
    d_att = (
        jnp.einsum("bld,ed->ble", d_branch, out_weight, preferred_element_type=jnp.float32)
        * keep[:, None, None]
    ).astype(jnp.bfloat16)
    all_d_att = from_blocks(
        lax.all_gather(d_att[None], ("vid", "txt"), axis=0, tiled=True), vid_count, txt_count
    )
    video_d_att = split_heads(take_rows(all_d_att, video_start, items_here))
    cap_d_att = split_heads(take_rows(all_d_att, cap_start, cap_items))
    video_dprobs = jnp.einsum(
        "blhe,bkhe->bhlk",
        video_d_att,
        split_heads(video_values),
        preferred_element_type=jnp.float32,
    )
    cap_dprobs = jnp.einsum(
        "blhe,bkhe->bhlk", cap_d_att, split_heads(cap_values), preferred_element_type=jnp.float32
    )
    delta_all = jnp.zeros((items_total, heads_here, lat_total), jnp.float32)
    delta_all = place_sum(delta_all, jnp.sum(video_probs * video_dprobs, axis=-1), video_start)
    delta_all = place_sum(delta_all, jnp.sum(cap_probs * cap_dprobs, axis=-1), cap_start)
    delta = lax.psum(delta_all, ("vid", "txt"))
    video_dscores = (
        video_probs * (video_dprobs - take_rows(delta, video_start, items_here)[..., None])
    ).astype(jnp.bfloat16)
    cap_dscores = (
        cap_probs * (cap_dprobs - take_rows(delta, cap_start, cap_items)[..., None])
    ).astype(jnp.bfloat16)
    video_dq = (
        jnp.einsum(
            "bhlk,bkhe->blhe",
            video_dscores,
            split_heads(video_keys),
            preferred_element_type=jnp.float32,
        )
        * scale
    ).reshape(items_here, lat_total, head_width)
    cap_dq = (
        jnp.einsum(
            "bhlk,bkhe->blhe",
            cap_dscores,
            split_heads(cap_keys),
            preferred_element_type=jnp.float32,
        )
        * scale
    ).reshape(cap_items, lat_total, head_width)
    query_all = jnp.zeros((items_total, lat_total, head_width), jnp.float32)
    query_all = place_sum(place_sum(query_all, video_dq, video_start), cap_dq, cap_start)
    d_queries = lax.psum_scatter(
        to_blocks(query_all, vid_count, txt_count), ("vid", "txt"), scatter_dimension=0, tiled=True
    )[0].astype(jnp.bfloat16)
    video_key_grad = (
        (
            jnp.einsum(
                "bhlk,blhe->bkhe",
                video_dscores,
                split_heads(video_queries),
                preferred_element_type=jnp.float32,
            )
            * scale
        )
        .reshape(items_here, video_here, head_width)
        .astype(jnp.bfloat16)
    )
    video_value_grad = (
        jnp.einsum("bhlk,blhe->bkhe", video_low, video_d_att, preferred_element_type=jnp.float32)
        .reshape(items_here, video_here, head_width)
        .astype(jnp.bfloat16)
    )
    caption_key_grad = (
        (
            jnp.einsum(
                "bhlk,blhe->bkhe",
                cap_dscores,
                split_heads(cap_queries),
                preferred_element_type=jnp.float32,
            )
            * scale
        )
        .reshape(cap_items, cap_here, head_width)
        .astype(jnp.bfloat16)
    )
    caption_value_grad = (
        jnp.einsum("bhlk,blhe->bkhe", cap_low, cap_d_att, preferred_element_type=jnp.float32)
        .reshape(cap_items, cap_here, head_width)
        .astype(jnp.bfloat16)
    )
    grad_query = jnp.einsum("bld,ble->de", lat_norm, d_queries, preferred_element_type=jnp.float32)
    d_lat_norm = lax.psum(
        jnp.einsum("ble,de->bld", d_queries, query_weight, preferred_element_type=jnp.float32),
        "head",
    )
    d_lat_back, grad_gain_latent = norm_back(lat_float, gain_latent, d_lat_norm)
    latent_grad = d_after + d_lat_back
    grad_key = jnp.einsum(
        "zsg,zsv->gv", video_normed, video_key_grad, preferred_element_type=jnp.float32
    ) + jnp.einsum(
        "zsg,zsv->gv", caption_normed, caption_key_grad, preferred_element_type=jnp.float32
    )
    grad_value = jnp.einsum(
        "zsg,zsv->gv", video_normed, video_value_grad, preferred_element_type=jnp.float32
    ) + jnp.einsum(
        "zsg,zsv->gv", caption_normed, caption_value_grad, preferred_element_type=jnp.float32
    )
    video_term = jnp.einsum(
        "ayt,ot->ayo", video_key_grad, key_matrix, preferred_element_type=jnp.float32
    ) + jnp.einsum(
        "ayt,ot->ayo", video_value_grad, value_matrix, preferred_element_type=jnp.float32
    )
    cap_term = jnp.einsum(
        "ayt,ot->ayo", caption_key_grad, key_matrix, preferred_element_type=jnp.float32
    ) + jnp.einsum(
        "ayt,ot->ayo", caption_value_grad, value_matrix, preferred_element_type=jnp.float32
    )
    d_video_norm, d_cap_norm = lax.psum((video_term, cap_term), "head")
    video_grad, video_gain_part = norm_back(video_float, gain_tokens, d_video_norm)
    caption_grad, cap_gain_part = norm_back(cap_float, gain_tokens, d_cap_norm)
    grad_gain_tokens = video_gain_part + cap_gain_part
    kept_here = jnp.sum(keep)
    (
        grad_query,
        grad_key,
        grad_value,
        grad_out,
        grad_up,
        grad_down,
        grad_gain_latent,
        grad_gain_tokens,
        grad_gain_mlp,
        kept_total,
    ) = lax.psum(
        (
            grad_query,
            grad_key,
            grad_value,
            grad_out,
            grad_up,
            grad_down,
            grad_gain_latent,
            grad_gain_tokens,
            grad_gain_mlp,
            kept_here,
        ),
        ("vid", "txt"),
    )
    kept_count = (kept_total / vid_count).astype(jnp.int32)
    return (
        latents_out,
        latent_grad,
        video_grad,
        caption_grad,
        grad_query,
        grad_key,
        grad_value,
        grad_out,
        grad_up,
        grad_down,
        grad_gain_latent,
        grad_gain_tokens,
        grad_gain_mlp,
        kept_count,
    )


def solution(mesh):
    in_specs = (
        P("txt", "vid", None),
        P("txt", "vid", None),
        P("vid", "txt", None),
        P("vid"),
        P("vid", "txt"),
        P("txt"),
        P(),
        P(),
        P(),
        P(None, "head"),
        P(None, "head"),
        P(None, "head"),
        P("head", None),
        P(None, "head"),
        P("head", None),
        P("txt", "vid", None),
    )
    out_specs = (
        P("txt", "vid", None),
        P("txt", "vid", None),
        P("txt", "vid", None),
        P("vid", "txt", None),
        P(None, "head"),
        P(None, "head"),
        P(None, "head"),
        P("head", None),
        P(None, "head"),
        P("head", None),
        P(),
        P(),
        P(),
        P(),
    )
    return jax.shard_map(local, mesh=mesh, in_specs=in_specs, out_specs=out_specs, check_vma=False)
```

profile of v0, /device:TPU:0, one launch (start us, length us, event | category | flops | bytes accessed | tf_op | source)
XLA Modules:
  0.0 1152.1 jit_solution(121106021653798068)
XLA Ops:
  13.7 3.7 convert_reduce_fusion
  19.3 4.8 fusion.13
  24.2 5.8 convolution_convert_fusion.1
  30.0 4.2 convolution_convert_fusion.2
  34.3 9.0 all-gather.5.cloned.1.call-done
  50.1 2.7 multiply_reduce_fusion.1
  57.6 24.3 %all_gather.25 = f32[8,32,3,128]{3,1,2,0:T(8,128)S(1)} all-gather(f32[1,32,3,128]{3,1,2,0:T(8,128)S(1)} %copy.109), channel_id=1, replica_groups=mesh['vid'=2,'txt'=4,'head'=4] {'vid','txt'}, dimensions={0}, use_global_device_ids=true | all-gather | bytes 442368 | tf_op jit(solution)/shard_map/all_gather | solution.py:12
  81.9 24.3 %all_gather.28 = f32[8,32,3,128]{3,1,2,0:T(8,128)S(1)} all-gather(f32[1,32,3,128]{3,1,2,0:T(8,128)S(1)} %copy.110), channel_id=1, replica_groups=mesh['vid'=2,'txt'=4,'head'=4] {'vid','txt'}, dimensions={0}, use_global_device_ids=true | all-gather | bytes 442368 | tf_op jit(solution)/shard_map/all_gather | solution.py:12
  108.2 4.3 fusion.33
  123.5 51.8 %reduce-scatter.3.cloned.1.call-done = f32[1,8,64,192]{3,2,1,0:T(8,128)} async-done(((f32[8,8,64,192]{3,2,1,0:T(8,128)}), f32[1,8,64,192]{3,2,1,0:T(8,128)}) %reduce-scatter.3.cloned.1.call-update) | async-done | bytes 393232 | tf_op jit(solution)/shard_map/reduce_scatter | solution.py:195
  178.0 69.3 %all-reduce.9.cloned.1.call-done = f32[8,64,768]{2,1,0:T(8,128)} async-done(((f32[8,64,768]{2,1,0:T(8,128)}), f32[8,64,768]{2,1,0:T(8,128)}) %all-reduce.9.cloned.1.call-update) | async-done | bytes 1572880 | tf_op jit(solution)/shard_map/psum | solution.py:199
  251.2 4.2 multiply_convert_fusion.2
  260.6 3.0 convolution_convert_fusion.3
  263.7 64.1 %all-reduce.13.cloned.1.call-done = f32[8,64,768]{2,1,0:T(8,128)} async-done(((f32[8,64,768]{2,1,0:T(8,128)}), f32[8,64,768]{2,1,0:T(8,128)}) %all-reduce.13.cloned.1.call-update) | async-done | bytes 1572880 | tf_op jit(solution)/shard_map/psum | solution.py:217
  330.4 43.3 %all-reduce.11.cloned.1.call-done = bf16[8,64,768]{2,1,0:T(8,128)(2,1)} async-done(((bf16[8,64,768]{2,1,0:T(8,128)(2,1)}), bf16[8,64,768]{2,1,0:T(8,128)(2,1)}) %all-reduce.11.cloned.1.call-update) | async-done | bytes 786448 | tf_op jit(solution)/shard_map/psum | solution.py:206
  373.6 3.1 fusion.116
  379.3 26.9 %all-gather.7.cloned.1.call-done = bf16[64,64,192]{2,1,0:T(8,128)(2,1)} async-done(((bf16[8,64,192]{2,1,0:T(8,128)(2,1)}), bf16[64,64,192]{2,1,0:T(8,128)(2,1)}) %all-gather.7.cloned.1.call-update) | async-done | bytes 1572880 | tf_op jit(solution)/shard_map/all_gather | solution.py:229
  410.6 5.8 multiply_reduce_fusion
  416.5 27.9 %psum.122 = f32[32,3,128]{2,1,0:T(4,128)S(1)} all-reduce(f32[32,3,128]{2,1,0:T(4,128)S(1)} %add_dynamic-update-slice_fusion.2), channel_id=1, replica_groups=mesh['vid'=2,'txt'=4,'head'=4] {'vid','txt'}, use_global_device_ids=true, to_apply=%region_22.23 | all-reduce | flops 12288 | bytes 98304 | tf_op jit(solution)/shard_map/psum | solution.py:245
  444.5 5.9 multiply_convert_fusion
  473.7 6.7 convolution_add_fusion
  480.4 32.0 %reduce-scatter.5.cloned.1.call-done = f32[1,8,64,192]{3,2,1,0:T(8,128)} async-done(((f32[8,8,64,192]{3,2,1,0:T(8,128)}), f32[1,8,64,192]{3,2,1,0:T(8,128)}) %reduce-scatter.5.cloned.1.call-update) | async-done | bytes 393232 | tf_op jit(solution)/shard_map/reduce_scatter | solution.py:272
  516.2 3.5 convolution_bitcast_fusion
  524.2 2.6 convolution_bitcast_fusion.2
  528.4 2.6 convolution_bitcast_fusion.3
  533.7 484.3 %all-reduce.17.cloned.1.call-done = (f32[8,64,768]{2,1,0:T(8,128)}, f32[8,512,768]{2,1,0:T(8,128)}, f32[16,16,768]{2,1,0:T(8,128)}) async-done(((f32[8,64,768]{2,1,0:T(8,128)}, f32[8,512,768]{2,1,0:T(8,128)}, f32[16,16,768]{2,1,0:T(8,128)}), (f32[8,64,768]{2,1,0:T(8,128)}, f32[8,512,768]{2,1,0:T(8,128)}, f32[16,16,768]{2,1,0:T(8,128)})) %all-reduce.17.cloned.1.call-update) | async-done | bytes 14942224 | tf_op jit(solution)/shard_map/psum | solution.py:312
  1019.4 10.0 fusion.14
  1032.1 6.6 fusion.12
  1040.6 28.1 %all-reduce = (f32[768]{0:T(1024)}, f32[768]{0:T(1024)}, f32[768]{0:T(1024)}, f32[]{:T(128)}) all-reduce(f32[768]{0:T(1024)S(1)} %get-tuple-element.163, f32[768]{0:T(1024)S(1)} %add.231, f32[768]{0:T(1024)S(1)} %copy-done.101, f32[]{:T(128)} %fusion.104), channel_id=1, replica_groups=mesh['vid'=2,'txt'=4,'head'=4] {'vid','txt'}, use_global_device_ids=true, to_apply=%region_40.41 | all-reduce | flops 2305 | bytes 18440 | tf_op jit(solution)/shard_map/psum | solution.py:354
  1071.9 3.5 add_add_fusion.3
  1075.4 10.8 broadcast_add_fusion
  1086.2 49.6 %all-reduce.15.cloned.1.call-done = (f32[768,192]{0,1:T(8,128)}, f32[768,192]{0,1:T(8,128)}, f32[768,192]{0,1:T(8,128)}, f32[192,768]{1,0:T(8,128)}, f32[768,768]{1,0:T(8,128)}, /*index=5*/f32[768,768]{1,0:T(8,128)}) async-done(((f32[768,192]{0,1:T(8,128)}, f32[768,192]{0,1:T(8,128)}, f32[768,192]{0,1:T(8,128)}, f32[192,768]{1,0:T(8,128)}, f32[768,768]{1,0:T(8,128)}, /*index=5*/f32[768,768]{1,0:T(8,128)}), ...) | async-done | bytes 7077904 | tf_op jit(solution)/shard_map/psum | solution.py:354
  (406 shorter events, 106.8 us)
Async XLA Ops:
  7.2 242.9 %copy-start = (bf16[768,768]{1,0:T(8,128)(2,1)S(1)}, bf16[768,768]{1,0:T(8,128)(2,1)}, u32[]{:S(2)}) copy-start(bf16[768,768]{1,0:T(8,128)(2,1)} %param.31) | copy-start | bytes 3538948
  7.2 36.0 %all-gather.5.cloned.1.call-start = ((), (), s32[]{:S(2)}) async-start(), calls=%async_computation.7 | async-start | bytes 2359296 | tf_op jit(solution)/shard_map/all_gather | solution.py:124
  12.6 162.7 %reduce-scatter.3.cloned.1.call-start = ((), (), s32[]{:S(2)}) async-start(), calls=%async_computation.2 | async-start | bytes 4718592 | tf_op jit(solution)/shard_map/reduce_scatter | solution.py:195
  19.1 36.4 %copy-start.32 = (bf16[16,16,3,64]{3,2,1,0:T(4,128)(2,1)}, bf16[16,16,3,64]{3,2,1,0:T(4,128)(2,1)S(1)}, u32[]{:S(2)}) copy-start(bf16[16,16,3,64]{3,2,1,0:T(4,128)(2,1)S(1)} %reshape.239) | copy-start | bytes 294916
  19.3 36.3 %copy-start.84 = (pred[16,16]{1,0:T(8,128)(4,1)}, pred[16,16]{1,0:T(8,128)(4,1)S(1)}, u32[]{:S(2)}) copy-start(pred[16,16]{1,0:T(8,128)(4,1)S(1)} %compare_and_fusion) | copy-start | bytes 772
  19.3 10.8 slice-start
  48.5 7.1 copy-start.18
  122.9 52.5 %copy-start.61 = (bf16[192,768]{1,0:T(8,128)(2,1)S(1)}, bf16[192,768]{1,0:T(8,128)(2,1)}, u32[]{:S(2)}) copy-start(bf16[192,768]{1,0:T(8,128)(2,1)} %param.30) | copy-start | bytes 884740
  122.9 124.4 %all-reduce.9.cloned.1.call-start = ((), (), s32[]{:S(2)}) async-start(), calls=%async_computation.3 | async-start | bytes 3145728 | tf_op jit(solution)/shard_map/psum | solution.py:199
  123.5 54.4 %copy-start.107 = (f32[8]{0:T(128)}, f32[8]{0:T(128)S(1)}, u32[]{:S(2)}) copy-start(f32[8]{0:T(128)S(1)} %subtract_convert_fusion) | copy-start | bytes 100
  178.0 149.8 %all-reduce.13.cloned.1.call-start = ((), (), s32[]{:S(2)}) async-start(), calls=%async_computation.5 | async-start | bytes 3145728 | tf_op jit(solution)/shard_map/psum | solution.py:217
  248.9 124.7 %copy-start.8 = (f32[8,64,768]{2,1,0:T(8,128)}, f32[8,64,768]{2,1,0:T(8,128)S(1)}, u32[]{:S(2)}) copy-start(f32[8,64,768]{2,1,0:T(8,128)S(1)} %get-tuple-element.199) | copy-start | bytes 4718596
  259.5 114.1 %all-reduce.11.cloned.1.call-start = ((), (), s32[]{:S(2)}) async-start(), calls=%async_computation.4 | async-start | bytes 1572864 | tf_op jit(solution)/shard_map/psum | solution.py:206
  260.6 67.2 %copy-start.82 = (f32[8,64]{1,0:T(8,128)S(1)}, f32[8,64]{1,0:T(8,128)}, u32[]{:S(2)}) copy-start(f32[8,64]{1,0:T(8,128)} %copy-done.81) | copy-start | bytes 6148
  260.6 67.2 %copy-start.99 = (f32[8,64]{1,0:T(8,128)S(1)}, f32[8,64]{1,0:T(8,128)}, u32[]{:S(2)}) copy-start(f32[8,64]{1,0:T(8,128)} %copy-done.98) | copy-start | bytes 6148
  260.6 67.2 %copy-start.103 = (f32[768]{0:T(1024)S(1)}, f32[768]{0:T(1024)}, u32[]{:S(2)}) copy-start(f32[768]{0:T(1024)} %param.26) | copy-start | bytes 9220
  263.6 66.7 %copy-start.97 = (f32[8,64]{1,0:T(8,128)S(1)}, f32[8,64]{1,0:T(8,128)}, u32[]{:S(2)}) copy-start(f32[8,64]{1,0:T(8,128)} %copy-done.96) | copy-start | bytes 6148
  263.6 142.5 %all-gather.7.cloned.1.call-start = ((), (), s32[]{:S(2)}) async-start(), calls=%async_computation.8 | async-start | bytes 2359296 | tf_op jit(solution)/shard_map/all_gather | solution.py:229
  377.9 30.0 %copy-start.45 = (bf16[8,64,768]{2,1,0:T(8,128)(2,1)}, bf16[8,64,768]{2,1,0:T(8,128)(2,1)S(1)}, u32[]{:S(2)}) copy-start(bf16[8,64,768]{2,1,0:T(8,128)(2,1)S(1)} %fusion.48) | copy-start | bytes 2359300
  379.0 133.4 %reduce-scatter.5.cloned.1.call-start = ((), (), s32[]{:S(2)}) async-start(), calls=%async_computation.6 | async-start | bytes 4718592 | tf_op jit(solution)/shard_map/reduce_scatter | solution.py:272
  409.0 7.4 copy-start.55
  461.1 557.0 %all-reduce.17.cloned.1.call-start = ((), (), s32[]{:S(2)}) async-start(), calls=%async_computation.10 | async-start | bytes 29884416 | tf_op jit(solution)/shard_map/psum | solution.py:312
  473.7 38.7 %copy-start.60 = (bf16[768,192]{0,1:T(8,128)(2,1)S(1)}, bf16[768,192]{0,1:T(8,128)(2,1)}, u32[]{:S(2)}) copy-start(bf16[768,192]{0,1:T(8,128)(2,1)} %param.27) | copy-start | bytes 884740
  514.9 8.7 slice-start.2
  514.9 620.9 %all-reduce.15.cloned.1.call-start = ((), (), s32[]{:S(2)}) async-start(), calls=%async_computation.9 | async-start | bytes 14155776 | tf_op jit(solution)/shard_map/psum | solution.py:354
  516.2 7.4 slice-start.3
  533.7 495.8 %slice-start.4 = ((s8[6291456]{0:T(1024)(128)(4,1)}), s8[2097152]{0:T(1024)(128)(4,1)S(1)}, s32[]{:S(2)}) async-start(s8[6291456]{0:T(1024)(128)(4,1)} %bitcast.180), calls=%async_computation.15 | async-start | bytes 4194304
  1019.4 10.0 copy-start.68
  1019.4 10.1 slice-start.5
  1019.4 12.7 %copy-start.2 = (f32[8,512,768]{2,1,0:T(8,128)S(1)}, f32[8,512,768]{2,1,0:T(8,128)}, u32[]{:S(2)}) copy-start(f32[8,512,768]{2,1,0:T(8,128)} %get-tuple-element.190) | copy-start | bytes 37748740
  1039.2 36.1 %slice-start.6 = ((s8[6291456]{0:T(1024)(128)(4,1)}), s8[2097152]{0:T(1024)(128)(4,1)S(1)}, s32[]{:S(2)}) async-start(s8[6291456]{0:T(1024)(128)(4,1)} %bitcast.182), calls=%async_computation.17 | async-start | bytes 4194304
  1040.6 31.3 %copy-start.93 = (f32[8,64]{1,0:T(8,128)S(1)}, f32[8,64]{1,0:T(8,128)}, u32[]{:S(2)}) copy-start(f32[8,64]{1,0:T(8,128)} %copy-done.92) | copy-start | bytes 6148
  (103 other events, 248.2 us)
Sparse Core Ops, SparseCore 0:
  12.7 30.4 all-gather.4
  123.0 52.2 reduce-scatter.2
  178.3 68.9 all-reduce.8
  259.6 68.1 all-reduce.12
  330.6 42.9 all-reduce.10
  379.1 27.0 all-gather.6
  461.2 51.1 reduce-scatter.4
  515.8 502.2 all-reduce.16
  1023.3 112.5 all-reduce.14
where the time goes:
time: 1160 us; the launch traced here: 1150 us
  waiting for transfers between devices  830 us (72%)
  blocking collectives  105 us (9%)
  matrix products  73.1 us (6%)
  other arithmetic  71.8 us (6%)
  local copies, waits for them, and re-layouts  53.3 us (5%)
  between operations  17.4 us (1%)
    psum x1, waiting for transfers between devices, local(): lax.psum(jnp.einsum('ble,de->bld', d_queries, query_weight, preferred_ele...  484 us
    psum x1, waiting for transfers between devices, local(): lax.psum(jnp.einsum('ble,ed->bld', mixed_in, out_weight, preferred_elemen...  69.3 us
    psum x1, waiting for transfers between devices, local(): lax.psum(jnp.einsum('blf,df->bld', d_pre, up_weight, preferred_element_ty...  64.1 us
    reduce_scatter x1, waiting for transfers between devices, local(): lax.psum_scatter(to_blocks(value_all, vid_count, txt_count), ('vid', 'txt...  51.8 us
    psum x1, waiting for transfers between devices, local(): lax.psum((grad_query, grad_key, grad_value, grad_out, grad_up, grad_down,...  49.6 us
    all_gather x2, blocking collectives, combined_all(): gathered = jax.tree.map(lambda a: lax.all_gather(a, axis), part)  48.6 us
    psum x1, waiting for transfers between devices, local(): lax.psum(jnp.einsum('blf,fd->bld', activ, down_weight, preferred_element_...  43.3 us
    reduce_scatter x1, waiting for transfers between devices, local(): lax.psum_scatter(to_blocks(query_all, vid_count, txt_count), ('vid', 'txt...  32 us
  transfers between devices with their start and end apart: 9, of which 9 were waited for; matrix products, arithmetic and copies ran while one was open for 8% of the time, Pallas kernels for 0%

commit v1 on v0

--- a/solution.py
+++ b/solution.py
@@ -1,3 +1,4 @@
+import functools
 import math
 import jax
 import jax.numpy as jnp
@@ -6,6 +7,14 @@
 
 D = 768
 HEADS = 12
+
+
+def use_map_now(x0, along_axis):
+    block_next = lax.all_gather(x0, axis_name=along_axis)
+    return jnp.sum(block_next, axis=0)
+
+
+form_the_slabs = functools.partial(use_map_now, along_axis="head")
 
 
 def combined_all(part, axis, combine):
@@ -196,8 +205,8 @@
         to_blocks(value_all, vid_count, txt_count), ("vid", "txt"), scatter_dimension=0, tiled=True
     )[0]
     mixed_in = (attended * keep[:, None, None]).astype(jnp.bfloat16)
-    branch = lax.psum(
-        jnp.einsum("ble,ed->bld", mixed_in, out_weight, preferred_element_type=jnp.float32), "head"
+    branch = form_the_slabs(
+        jnp.einsum("ble,ed->bld", mixed_in, out_weight, preferred_element_type=jnp.float32)
     )
     after_attn = lat_float + branch
     mlp_norm = layer_norm(after_attn, gain_mlp).astype(jnp.bfloat16)

time: 1160 us -> 1210 us (1.043)
  waiting for transfers between devices: 830 us -> 876 us
    all_gather x0 -> x1, waiting for transfers between devices: none -> 115 us  [use_map_now(): block_next = lax.all_gather(x0, axis_name=along_axis)]
    psum x1 -> x0, waiting for transfers between devices: 69.3 us -> none  [local(): lax.psum(jnp.einsum('ble,ed->bld', mixed_in, out_weight, preferred_elemen...]
where the time goes in v1:
time: 1210 us; the launch traced here: 1200 us
  waiting for transfers between devices  876 us (72%)
  blocking collectives  105 us (9%)
  other arithmetic  76.3 us (6%)
  matrix products  73.1 us (6%)
  local copies, waits for them, and re-layouts  53.3 us (4%)
  between operations  17.4 us (1%)
    psum x1, waiting for transfers between devices, local(): lax.psum(jnp.einsum('ble,de->bld', d_queries, query_weight, preferred_ele...  484 us
    all_gather x1, waiting for transfers between devices, use_map_now(): block_next = lax.all_gather(x0, axis_name=along_axis)  115 us
    psum x1, waiting for transfers between devices, local(): lax.psum(jnp.einsum('blf,df->bld', d_pre, up_weight, preferred_element_ty...  63.1 us
    reduce_scatter x1, waiting for transfers between devices, local(): lax.psum_scatter(to_blocks(value_all, vid_count, txt_count), ('vid', 'txt...  51.8 us
    psum x1, waiting for transfers between devices, local(): lax.psum((grad_query, grad_key, grad_value, grad_out, grad_up, grad_down,...  49.6 us
    all_gather x2, blocking collectives, combined_all(): gathered = jax.tree.map(lambda a: lax.all_gather(a, axis), part)  48.6 us
    psum x1, waiting for transfers between devices, local(): lax.psum(jnp.einsum('blf,fd->bld', activ, down_weight, preferred_element_...  43.3 us
    reduce_scatter x1, waiting for transfers between devices, local(): lax.psum_scatter(to_blocks(query_all, vid_count, txt_count), ('vid', 'txt...  32 us
  transfers between devices with their start and end apart: 9, of which 9 were waited for; matrix products, arithmetic and copies ran while one was open for 8% of the time, Pallas kernels for 0%

profile of v1, /device:TPU:0, one launch (start us, length us, event | category | flops | bytes accessed | tf_op | source)
XLA Modules:
  0.0 1201.8 jit_solution(16902197407053476876)
XLA Ops:
  13.7 3.7 convert_reduce_fusion
  19.3 4.8 fusion.13
  24.2 5.8 convolution_convert_fusion.1
  30.0 4.2 convolution_convert_fusion.2
  34.3 9.0 all-gather.7.cloned.1.call-done
  50.1 2.7 multiply_reduce_fusion.1
  57.6 24.3 %all_gather.31 = f32[8,32,3,128]{3,1,2,0:T(8,128)S(1)} all-gather(f32[1,32,3,128]{3,1,2,0:T(8,128)S(1)} %copy.109), channel_id=1, replica_groups=mesh['vid'=2,'txt'=4,'head'=4] {'vid','txt'}, dimensions={0}, use_global_device_ids=true | all-gather | bytes 442368 | tf_op jit(solution)/shard_map/all_gather | solution.py:21
  81.9 24.3 %all_gather.34 = f32[8,32,3,128]{3,1,2,0:T(8,128)S(1)} all-gather(f32[1,32,3,128]{3,1,2,0:T(8,128)S(1)} %copy.110), channel_id=1, replica_groups=mesh['vid'=2,'txt'=4,'head'=4] {'vid','txt'}, dimensions={0}, use_global_device_ids=true | all-gather | bytes 442368 | tf_op jit(solution)/shard_map/all_gather | solution.py:21
  108.2 4.3 fusion.33
  123.5 51.8 %reduce-scatter.3.cloned.1.call-done = f32[1,8,64,192]{3,2,1,0:T(8,128)} async-done(((f32[8,8,64,192]{3,2,1,0:T(8,128)}), f32[1,8,64,192]{3,2,1,0:T(8,128)}) %reduce-scatter.3.cloned.1.call-update) | async-done | bytes 393232 | tf_op jit(solution)/shard_map/reduce_scatter | solution.py:204
  178.0 115.4 %all-gather.9.cloned.1.call-done = f32[32,64,768]{2,1,0:T(8,128)} async-done(((f32[8,64,768]{2,1,0:T(8,128)}), f32[32,64,768]{2,1,0:T(8,128)}) %all-gather.9.cloned.1.call-update) | async-done | bytes 6291472 | tf_op jit(solution)/shard_map/all_gather | solution.py:13
  293.4 4.5 reduce_sum.240
  301.8 4.2 multiply_convert_fusion.2
  311.3 3.0 convolution_convert_fusion.3
  314.3 63.1 %all-reduce.10.cloned.1.call-done = f32[8,64,768]{2,1,0:T(8,128)} async-done(((f32[8,64,768]{2,1,0:T(8,128)}), f32[8,64,768]{2,1,0:T(8,128)}) %all-reduce.10.cloned.1.call-update) | async-done | bytes 1572880 | tf_op jit(solution)/shard_map/psum | solution.py:226
  380.0 43.3 %all-reduce.8.cloned.1.call-done = bf16[8,64,768]{2,1,0:T(8,128)(2,1)} async-done(((bf16[8,64,768]{2,1,0:T(8,128)(2,1)}), bf16[8,64,768]{2,1,0:T(8,128)(2,1)}) %all-reduce.8.cloned.1.call-update) | async-done | bytes 786448 | tf_op jit(solution)/shard_map/psum | solution.py:215
  423.3 3.1 fusion.116
  428.9 26.9 %all-gather.11.cloned.1.call-done = bf16[64,64,192]{2,1,0:T(8,128)(2,1)} async-done(((bf16[8,64,192]{2,1,0:T(8,128)(2,1)}), bf16[64,64,192]{2,1,0:T(8,128)(2,1)}) %all-gather.11.cloned.1.call-update) | async-done | bytes 1572880 | tf_op jit(solution)/shard_map/all_gather | solution.py:238
  460.3 5.8 multiply_reduce_fusion
  466.2 27.9 %psum.114 = f32[32,3,128]{2,1,0:T(4,128)S(1)} all-reduce(f32[32,3,128]{2,1,0:T(4,128)S(1)} %add_dynamic-update-slice_fusion.2), channel_id=1, replica_groups=mesh['vid'=2,'txt'=4,'head'=4] {'vid','txt'}, use_global_device_ids=true, to_apply=%region_22.23 | all-reduce | flops 12288 | bytes 98304 | tf_op jit(solution)/shard_map/psum | solution.py:254
  494.2 5.9 multiply_convert_fusion
  523.3 6.7 convolution_add_fusion
  530.1 32.0 %reduce-scatter.5.cloned.1.call-done = f32[1,8,64,192]{3,2,1,0:T(8,128)} async-done(((f32[8,8,64,192]{3,2,1,0:T(8,128)}), f32[1,8,64,192]{3,2,1,0:T(8,128)}) %reduce-scatter.5.cloned.1.call-update) | async-done | bytes 393232 | tf_op jit(solution)/shard_map/reduce_scatter | solution.py:281
  565.9 3.5 convolution_bitcast_fusion
  573.9 2.6 convolution_bitcast_fusion.2
  583.4 484.3 %all-reduce.14.cloned.1.call-done = (f32[8,64,768]{2,1,0:T(8,128)}, f32[8,512,768]{2,1,0:T(8,128)}, f32[16,16,768]{2,1,0:T(8,128)}) async-done(((f32[8,64,768]{2,1,0:T(8,128)}, f32[8,512,768]{2,1,0:T(8,128)}, f32[16,16,768]{2,1,0:T(8,128)}), (f32[8,64,768]{2,1,0:T(8,128)}, f32[8,512,768]{2,1,0:T(8,128)}, f32[16,16,768]{2,1,0:T(8,128)})) %all-reduce.14.cloned.1.call-update) | async-done | bytes 14942224 | tf_op jit(solution)/shard_map/psum | solution.py:321
  1069.1 10.0 fusion.14
  1081.8 6.6 fusion.12
  1090.3 28.1 %all-reduce = (f32[768]{0:T(1024)}, f32[768]{0:T(1024)}, f32[768]{0:T(1024)}, f32[]{:T(128)}) all-reduce(f32[768]{0:T(1024)S(1)} %get-tuple-element.163, f32[768]{0:T(1024)S(1)} %add.229, f32[768]{0:T(1024)S(1)} %copy-done.101, f32[]{:T(128)} %fusion.104), channel_id=1, replica_groups=mesh['vid'=2,'txt'=4,'head'=4] {'vid','txt'}, use_global_device_ids=true, to_apply=%region_40.41 | all-reduce | flops 2305 | bytes 18440 | tf_op jit(solution)/shard_map/psum | solution.py:363
  1121.6 3.5 add_add_fusion.3
  1125.1 10.8 broadcast_add_fusion
  1135.9 49.6 %all-reduce.12.cloned.1.call-done = (f32[768,192]{0,1:T(8,128)}, f32[768,192]{0,1:T(8,128)}, f32[768,192]{0,1:T(8,128)}, f32[192,768]{1,0:T(8,128)}, f32[768,768]{1,0:T(8,128)}, /*index=5*/f32[768,768]{1,0:T(8,128)}) async-done(((f32[768,192]{0,1:T(8,128)}, f32[768,192]{0,1:T(8,128)}, f32[768,192]{0,1:T(8,128)}, f32[192,768]{1,0:T(8,128)}, f32[768,768]{1,0:T(8,128)}, /*index=5*/f32[768,768]{1,0:T(8,128)}), ...) | async-done | bytes 7077904 | tf_op jit(solution)/shard_map/psum | solution.py:363
  (407 shorter events, 109.4 us)
Async XLA Ops:
  7.2 293.5 %copy-start = (bf16[768,768]{1,0:T(8,128)(2,1)S(1)}, bf16[768,768]{1,0:T(8,128)(2,1)}, u32[]{:S(2)}) copy-start(bf16[768,768]{1,0:T(8,128)(2,1)} %param.31) | copy-start | bytes 3538948
  7.2 36.0 %all-gather.7.cloned.1.call-start = ((), (), s32[]{:S(2)}) async-start(), calls=%async_computation.6 | async-start | bytes 2359296 | tf_op jit(solution)/shard_map/all_gather | solution.py:133
  12.6 162.7 %reduce-scatter.3.cloned.1.call-start = ((), (), s32[]{:S(2)}) async-start(), calls=%async_computation.2 | async-start | bytes 4718592 | tf_op jit(solution)/shard_map/reduce_scatter | solution.py:204
  19.1 36.4 %copy-start.32 = (bf16[16,16,3,64]{3,2,1,0:T(4,128)(2,1)}, bf16[16,16,3,64]{3,2,1,0:T(4,128)(2,1)S(1)}, u32[]{:S(2)}) copy-start(bf16[16,16,3,64]{3,2,1,0:T(4,128)(2,1)S(1)} %reshape.239) | copy-start | bytes 294916
  19.3 36.3 %copy-start.84 = (pred[16,16]{1,0:T(8,128)(4,1)}, pred[16,16]{1,0:T(8,128)(4,1)S(1)}, u32[]{:S(2)}) copy-start(pred[16,16]{1,0:T(8,128)(4,1)S(1)} %compare_and_fusion) | copy-start | bytes 772
  19.3 10.8 slice-start
  48.5 7.1 copy-start.18
  122.9 52.5 %copy-start.61 = (bf16[192,768]{1,0:T(8,128)(2,1)S(1)}, bf16[192,768]{1,0:T(8,128)(2,1)}, u32[]{:S(2)}) copy-start(bf16[192,768]{1,0:T(8,128)(2,1)} %param.30) | copy-start | bytes 884740
  122.9 170.5 %all-gather.9.cloned.1.call-start = ((), (), s32[]{:S(2)}) async-start(), calls=%async_computation.7 | async-start | bytes 7864320 | tf_op jit(solution)/shard_map/all_gather | solution.py:13
  123.5 54.4 %copy-start.107 = (f32[8]{0:T(128)}, f32[8]{0:T(128)S(1)}, u32[]{:S(2)}) copy-start(f32[8]{0:T(128)S(1)} %subtract_convert_fusion) | copy-start | bytes 100
  178.0 199.5 %all-reduce.10.cloned.1.call-start = ((), (), s32[]{:S(2)}) async-start(), calls=%async_computation.4 | async-start | bytes 3145728 | tf_op jit(solution)/shard_map/psum | solution.py:226
  299.6 123.7 %copy-start.8 = (f32[8,64,768]{2,1,0:T(8,128)}, f32[8,64,768]{2,1,0:T(8,128)S(1)}, u32[]{:S(2)}) copy-start(f32[8,64,768]{2,1,0:T(8,128)S(1)} %get-tuple-element.199) | copy-start | bytes 4718596
  310.2 113.1 %all-reduce.8.cloned.1.call-start = ((), (), s32[]{:S(2)}) async-start(), calls=%async_computation.3 | async-start | bytes 1572864 | tf_op jit(solution)/shard_map/psum | solution.py:215
  311.3 66.2 %copy-start.82 = (f32[8,64]{1,0:T(8,128)S(1)}, f32[8,64]{1,0:T(8,128)}, u32[]{:S(2)}) copy-start(f32[8,64]{1,0:T(8,128)} %copy-done.81) | copy-start | bytes 6148
  311.3 66.2 %copy-start.99 = (f32[8,64]{1,0:T(8,128)S(1)}, f32[8,64]{1,0:T(8,128)}, u32[]{:S(2)}) copy-start(f32[8,64]{1,0:T(8,128)} %copy-done.98) | copy-start | bytes 6148
  311.3 66.2 %copy-start.103 = (f32[768]{0:T(1024)S(1)}, f32[768]{0:T(1024)}, u32[]{:S(2)}) copy-start(f32[768]{0:T(1024)} %param.26) | copy-start | bytes 9220
  314.3 65.8 %copy-start.97 = (f32[8,64]{1,0:T(8,128)S(1)}, f32[8,64]{1,0:T(8,128)}, u32[]{:S(2)}) copy-start(f32[8,64]{1,0:T(8,128)} %copy-done.96) | copy-start | bytes 6148
  314.3 141.6 %all-gather.11.cloned.1.call-start = ((), (), s32[]{:S(2)}) async-start(), calls=%async_computation.8 | async-start | bytes 2359296 | tf_op jit(solution)/shard_map/all_gather | solution.py:238
  427.6 30.0 %copy-start.45 = (bf16[8,64,768]{2,1,0:T(8,128)(2,1)}, bf16[8,64,768]{2,1,0:T(8,128)(2,1)S(1)}, u32[]{:S(2)}) copy-start(bf16[8,64,768]{2,1,0:T(8,128)(2,1)S(1)} %fusion.48) | copy-start | bytes 2359300
  428.7 133.4 %reduce-scatter.5.cloned.1.call-start = ((), (), s32[]{:S(2)}) async-start(), calls=%async_computation.5 | async-start | bytes 4718592 | tf_op jit(solution)/shard_map/reduce_scatter | solution.py:281
  458.7 7.4 copy-start.55
  510.7 557.0 %all-reduce.14.cloned.1.call-start = ((), (), s32[]{:S(2)}) async-start(), calls=%async_computation.10 | async-start | bytes 29884416 | tf_op jit(solution)/shard_map/psum | solution.py:321
  523.3 38.7 %copy-start.60 = (bf16[768,192]{0,1:T(8,128)(2,1)S(1)}, bf16[768,192]{0,1:T(8,128)(2,1)}, u32[]{:S(2)}) copy-start(bf16[768,192]{0,1:T(8,128)(2,1)} %param.27) | copy-start | bytes 884740
  564.6 8.7 slice-start.2
  564.6 620.9 %all-reduce.12.cloned.1.call-start = ((), (), s32[]{:S(2)}) async-start(), calls=%async_computation.9 | async-start | bytes 14155776 | tf_op jit(solution)/shard_map/psum | solution.py:363
  565.9 7.4 slice-start.3
  583.3 495.8 %slice-start.4 = ((s8[6291456]{0:T(1024)(128)(4,1)}), s8[2097152]{0:T(1024)(128)(4,1)S(1)}, s32[]{:S(2)}) async-start(s8[6291456]{0:T(1024)(128)(4,1)} %bitcast.181), calls=%async_computation.15 | async-start | bytes 4194304
  1069.1 10.0 copy-start.68
  1069.1 10.1 slice-start.5
  1069.1 12.7 %copy-start.2 = (f32[8,512,768]{2,1,0:T(8,128)S(1)}, f32[8,512,768]{2,1,0:T(8,128)}, u32[]{:S(2)}) copy-start(f32[8,512,768]{2,1,0:T(8,128)} %get-tuple-element.190) | copy-start | bytes 37748740
  1088.9 36.1 %slice-start.6 = ((s8[6291456]{0:T(1024)(128)(4,1)}), s8[2097152]{0:T(1024)(128)(4,1)S(1)}, s32[]{:S(2)}) async-start(s8[6291456]{0:T(1024)(128)(4,1)} %bitcast.183), calls=%async_computation.17 | async-start | bytes 4194304
  1090.3 31.3 %copy-start.93 = (f32[8,64]{1,0:T(8,128)S(1)}, f32[8,64]{1,0:T(8,128)}, u32[]{:S(2)}) copy-start(f32[8,64]{1,0:T(8,128)} %copy-done.92) | copy-start | bytes 6148
  (103 other events, 248.2 us)
Sparse Core Ops, SparseCore 0:
  12.7 30.4 all-gather.6
  123.0 52.2 reduce-scatter.2
  178.1 115.3 all-gather.8
  310.3 67.1 all-reduce.9
  380.3 42.9 all-reduce.7
  428.8 27.0 all-gather.10
  510.9 51.1 reduce-scatter.4
  565.4 502.2 all-reduce.13
  1072.9 112.5 all-reduce.11
